TPU v7x, 32 devices: a whole 2x2x4 slice. The times are simulated.
32 devices in a mesh: rep: 2 (over y), fsdp: 4 (over z), section: 4 (over x, core).
Axes of the slice: x: 2, y: 2, z: 4, core: 2. Of those that a mesh axis runs over, the one named last changes fastest.
Arguments:
- iterate: bfloat16 [8, 3072, 1024], P(('rep', 'section'), None, 'fsdp'), parts along dimension 0, may hold values from -0.1875 to 0.1875
Outputs:
- update: bfloat16 [8, 3072, 1024], P(('rep', 'section'), None, 'fsdp'), parts along dimension 0
There are 2 independent parts, one for each index of `rep`. A program takes and returns all parts, laid end to end along the dimension named above; each array names one. Nothing has to cross between parts.
All inputs are finite; a program needn't handle non-finite values.
Results may differ from a plain program's by a relative error of at most 0.0055.
Values may be sent and summed in bfloat16 or wider, within the bound.
A program may use at most 128 MiB of HBM per device.

v0:
```python
import math
import jax
import jax.numpy as jnp
import numpy as np
from jax import lax
from jax.sharding import PartitionSpec as P


def tile_table(devices, band_blocks):
    block_table = np.zeros((devices, devices), dtype=np.int32)
    for row_block in range(devices):
        for col_block in range(devices):
            distance = (col_block - row_block) % devices
            if distance <= devices // 2:
                block_table[row_block, col_block] = row_block * band_blocks + distance
            else:
                block_table[row_block, col_block] = (
                    devices * band_blocks + col_block * band_blocks + (devices - distance)
                )
    return block_table


def on_device(iterate):
    devices = lax.axis_size("fsdp")
    experts, rows_all, columns = iterate.shape
    strip_rows = rows_all // devices
    band_blocks = devices // 2 + 1
    out_scale = 0.2 * math.sqrt(max(rows_all, columns * devices))
    expert_rows = iterate[0]
    row_blocks = expert_rows.reshape(devices, strip_rows, columns)

    def one_offset(offset):
        partner = jnp.roll(row_blocks, -offset, axis=0)
        tiles = jnp.einsum("nsc,ntc->nst", row_blocks, partner, preferred_element_type=jnp.float32)
        return tiles.astype(jnp.bfloat16)

    band_term = lax.map(one_offset, jnp.arange(band_blocks, dtype=jnp.int32))
    received = lax.all_to_all(band_term, "fsdp", split_axis=1, concat_axis=1, tiled=True)
    own_band = jnp.sum(received.astype(jnp.float32), axis=1).astype(jnp.bfloat16)
    upper_tiles = lax.all_gather(own_band, "fsdp", axis=0, tiled=True)
    tile_pool = jnp.concatenate([upper_tiles, jnp.swapaxes(upper_tiles, 1, 2)], axis=0)
    block_table = jnp.asarray(tile_table(devices, band_blocks))
    dense_blocks = jnp.take(tile_pool, block_table, axis=0)

    def apply_gram(operand):
        shaped = operand.reshape(devices, strip_rows, columns)
        product = jnp.einsum(
            "nmij,mjc->nic", dense_blocks, shaped, preferred_element_type=jnp.float32
        )
        return product.reshape(rows_all, columns)

    first_product = apply_gram(expert_rows)
    second_product = apply_gram(first_product.astype(jnp.bfloat16))
    combined = out_scale * (
        3.4445 * expert_rows.astype(jnp.float32) - 4.775 * first_product + 2.0315 * second_product
    )
    results = [combined.astype(jnp.bfloat16)]
    return jnp.stack(results)


def on_device_columns(iterate):
    devices = lax.axis_size("fsdp")
    own = lax.axis_index("fsdp")
    _, rows_all, columns = iterate.shape
    out_scale = 0.2 * math.sqrt(max(rows_all, columns * devices))
    gathered = lax.all_gather(iterate[0], "fsdp", axis=1, tiled=True)
    gram = lax.dot_general(
        gathered, gathered, (((0,), (0,)), ((), ())), preferred_element_type=jnp.float32
    )
    gram_half = gram.astype(jnp.bfloat16)
    own_gram = lax.dynamic_slice_in_dim(gram, own * columns, columns, 1)
    square = jnp.dot(gram_half, own_gram.astype(jnp.bfloat16), preferred_element_type=jnp.float32)
    row_ids = lax.broadcasted_iota(jnp.int32, square.shape, 0)
    column_ids = lax.broadcasted_iota(jnp.int32, square.shape, 1) + own * columns
    identity = (row_ids == column_ids).astype(jnp.float32)
    mixing = out_scale * (3.4445 * identity - 4.775 * own_gram + 2.0315 * square)
    update = jnp.dot(gathered, mixing.astype(jnp.bfloat16), preferred_element_type=jnp.float32)
    return update.astype(jnp.bfloat16)[None]


def for_shapes(iterate):
    _, rows_all, columns = iterate.shape
    if columns * lax.axis_size("fsdp") <= rows_all:
        return on_device_columns(iterate)
    return on_device(iterate)


def solution(mesh):
    return jax.shard_map(
        for_shapes,
        mesh=mesh,
        in_specs=(P(("rep", "section"), None, "fsdp"),),
        out_specs=P(("rep", "section"), None, "fsdp"),
        check_vma=False,
    )
```

profile of v0, /device:TPU:0, one launch (start us, length us, event | category | flops | bytes accessed | tf_op | source)
XLA Modules:
  0.0 155.0 jit_solution(9944123637097311542)
XLA Ops:
  6.5 0.0 all-gather.3.cloned.1.call-start
  6.5 0.7 all-gather.3.cloned.1.call-update
  7.3 119.2 %all-gather.3.cloned.1.call-done = bf16[1,3072,1024]{2,1,0:T(8,128)(2,1)} async-done(((bf16[1,3072,256]{2,1,0:T(8,128)(2,1)}), bf16[1,3072,1024]{2,1,0:T(8,128)(2,1)}) %all-gather.3.cloned.1.call-update) | async-done | bytes 6291472 | tf_op jit(solution)/shard_map/all_gather | solution.py:66
  126.5 12.0 %fusion.2 = f32[1024,1024]{1,0:T(8,128)} fusion(bf16[1,3072,1024]{2,1,0:T(8,128)(2,1)} %all-gather.3.cloned.1.call-done), kind=kOutput, calls=%fused_computation.2 | convolution fusion | flops 6442450944 | bytes 10485760 | tf_op jit(solution)/shard_map/dot_general | solution.py:67
  138.5 8.1 %fusion.7 = bf16[1,3072,256]{1,2,0:T(8,128)(2,1)S(1)} fusion(bf16[1,3072,1024]{2,1,0:T(8,128)(2,1)} %all-gather.3.cloned.1.call-done, f32[1024,1024]{1,0:T(8,128)} %fusion.2, s32[]{:T(128)S(6)} %select_n.3, s32[256]{0:T(256)S(1)} %iota_add_fusion), kind=kOutput, calls=%fused_computation.5 | convolution fusion | flops 2151677952 | bytes 14157824 | tf_op jit(solution)/shard_map/dot_general | solution.py:77
  146.6 1.6 %copy.2 = bf16[1,3072,256]{2,1,0:T(8,128)(2,1)} copy(bf16[1,3072,256]{1,2,0:T(8,128)(2,1)S(1)} %fusion.7) | data formatting | bytes 3145728 | tf_op jit(solution)/shard_map/broadcast_in_dim | solution.py:78
  (1 shorter events, 0.0 us)
Async XLA Ops:
  6.5 120.0 %all-gather.3.cloned.1.call-start = ((), (), s32[]{:S(2)}) async-start(), calls=%async_computation | async-start | bytes 7864320 | tf_op jit(solution)/shard_map/all_gather | solution.py:66
Sparse Core Ops, SparseCore 0:
  8.9 117.5 all-gather.2
where the time goes:
time: 155 us
  waiting for transfers between devices  120 us (77%)
  matrix products  20.1 us (13%)
  between operations  13.4 us (9%)
  local copies, waits for them, and re-layouts  1.57 us (1%)
    all_gather x1, waiting for transfers between devices, on_device_columns(): gathered = lax.all_gather(iterate[0], 'fsdp', axis=1, tiled=True)  119 us
    dot_general x1, matrix products, on_device_columns(): lax.dot_general(gathered, gathered, (((0,), (0,)), ((), ())), preferred_e...  12 us
    dot_general x1, matrix products, on_device_columns(): jnp.dot(gathered, mixing.astype(jnp.bfloat16), preferred_element_type=jnp...  8.06 us
  transfers between devices with their start and end apart: 1, of which 1 were waited for; matrix products, arithmetic and copies ran while one was open for 0% of the time, Pallas kernels for 0%

commit v1 on v0

--- a/solution.py
+++ b/solution.py
@@ -63,7 +63,12 @@
     own = lax.axis_index("fsdp")
     _, rows_all, columns = iterate.shape
     out_scale = 0.2 * math.sqrt(max(rows_all, columns * devices))
-    gathered = lax.all_gather(iterate[0], "fsdp", axis=1, tiled=True)
+    ring = [iterate[0]]
+    for hop in range(3):
+        ring.append(lax.ppermute(ring[-1], "fsdp", [(dev, (dev + 1) % 4) for dev in range(4)]))
+    gathered = jnp.roll(
+        jnp.concatenate(ring[::-1], axis=1), (lax.axis_index("fsdp") + 1) * ring[0].shape[1], axis=1
+    )
     gram = lax.dot_general(
         gathered, gathered, (((0,), (0,)), ((), ())), preferred_element_type=jnp.float32
     )

time: 155 us -> 145 us (0.935)
  between operations: 13.4 us -> 0.09 us
  local copies, waits for them, and re-layouts: 1.57 us -> 13.3 us
  waiting for transfers between devices: 120 us -> 111 us
  starting transfers between devices: 0.01 us -> 3.03 us
  matrix products: 20.1 us -> 17.7 us
    all_gather x1 -> x0, waiting for transfers between devices: 119 us -> none  [on_device_columns(): gathered = lax.all_gather(iterate[0], 'fsdp', axis=1, tiled=True)]
    ppermute x0 -> x3, waiting for transfers between devices: none -> 111 us  [on_device_columns(): lax.ppermute(ring[-1], 'fsdp', [(dev, (dev + 1) % 4) for dev in range(4)])]
    unnamed x0 -> x11, local copies, waits for them, and re-layouts: none -> 13.1 us
    dot_general x1, matrix products: 12 us -> 8.32 us  [on_device_columns(): lax.dot_general(gathered, gathered, (((0,), (0,)), ((), ())), preferred_e...]
    ppermute x0 -> x3, starting transfers between devices: none -> 3.03 us  [on_device_columns(): lax.ppermute(ring[-1], 'fsdp', [(dev, (dev + 1) % 4) for dev in range(4)])]
    broadcast_in_dim x1 -> x0, local copies, waits for them, and re-layouts: 1.57 us -> none  [on_device_columns(): return update.astype(jnp.bfloat16)[None]]
  transfers between devices with their start and end apart: 1 -> 3, of which waited for: 1 -> 3; matrix products, arithmetic and copies ran while one was open for 0% -> 0% of each run, Pallas kernels for 0% -> 0%
where the time goes in v1:
time: 145 us
  waiting for transfers between devices  111 us (77%)
  matrix products  17.7 us (12%)
  local copies, waits for them, and re-layouts  13.3 us (9%)
  starting transfers between devices  3.03 us (2%)
    ppermute x3, waiting for transfers between devices, on_device_columns(): lax.ppermute(ring[-1], 'fsdp', [(dev, (dev + 1) % 4) for dev in range(4)])  111 us
    unnamed x11, local copies, waits for them, and re-layouts  13.1 us
    dot_general x1, matrix products, on_device_columns(): jnp.dot(gathered, mixing.astype(jnp.bfloat16), preferred_element_type=jnp...  9.38 us
    dot_general x1, matrix products, on_device_columns(): lax.dot_general(gathered, gathered, (((0,), (0,)), ((), ())), preferred_e...  8.32 us
    ppermute x3, starting transfers between devices, on_device_columns(): lax.ppermute(ring[-1], 'fsdp', [(dev, (dev + 1) % 4) for dev in range(4)])  3.03 us
  transfers between devices with their start and end apart: 3, of which 3 were waited for; matrix products, arithmetic and copies ran while one was open for 0% of the time, Pallas kernels for 0%

profile of v1, /device:TPU:0, one launch (start us, length us, event | category | flops | bytes accessed | tf_op | source)
XLA Modules:
  0.0 145.1 jit_solution(10046744494581657002)
XLA Ops:
  0.0 0.0 copy-start
  0.0 3.0 %collective-permute-start = (bf16[3072,256]{1,0:T(8,128)(2,1)}, bf16[3072,256]{1,0:T(8,128)(2,1)S(1)}, u32[]{:S(2)}, u32[]{:S(2)}) collective-permute-start(bf16[3072,256]{1,0:T(8,128)(2,1)} %bitcast.5), channel_id=1, source_target_pairs={{0,4},{4,8},{8,12},{12,0},{1,5},{5,9},{9,13},{13,1},{2,6},{6,10},{... | collective-permute-start | bytes 4718600 | tf_op jit(solution)/shard_map/ppermute | solution.py:68
  3.0 36.7 %collective-permute-done = bf16[3072,256]{1,0:T(8,128)(2,1)S(1)} collective-permute-done((bf16[3072,256]{1,0:T(8,128)(2,1)}, bf16[3072,256]{1,0:T(8,128)(2,1)S(1)}, u32[]{:S(2)}, u32[]{:S(2)}) %collective-permute-start) | collective-permute-done | bytes 1572896 | tf_op jit(solution)/shard_map/ppermute | solution.py:68
  39.7 0.0 collective-permute-start.1
  39.7 37.5 %collective-permute-done.1 = bf16[3072,256]{1,0:T(8,128)(2,1)} collective-permute-done((bf16[3072,256]{1,0:T(8,128)(2,1)S(1)}, bf16[3072,256]{1,0:T(8,128)(2,1)}, u32[]{:S(2)}, u32[]{:S(2)}) %collective-permute-start.1) | collective-permute-done | bytes 1572896 | tf_op jit(solution)/shard_map/ppermute | solution.py:68
  77.2 0.0 collective-permute-start.2
  77.2 36.8 %collective-permute-done.2 = bf16[3072,256]{1,0:T(8,128)(2,1)} collective-permute-done((bf16[3072,256]{1,0:T(8,128)(2,1)}, bf16[3072,256]{1,0:T(8,128)(2,1)}, u32[]{:S(2)}, u32[]{:S(2)}) %collective-permute-start.2) | collective-permute-done | bytes 1572896 | tf_op jit(solution)/shard_map/ppermute | solution.py:68
  114.0 1.6 %constant_dynamic-update-slice_fusion.7 = bf16[3072,2048]{1,0:T(8,128)(2,1)S(1)} fusion(bf16[3072,256]{1,0:T(8,128)(2,1)} %collective-permute-done.2), kind=kLoop, calls=%fused_computation.23 | loop fusion | bytes 3145728
  115.6 1.6 %constant_dynamic-update-slice_fusion.6 = bf16[3072,2048]{1,0:T(8,128)(2,1)S(1)} fusion(bf16[3072,2048]{1,0:T(8,128)(2,1)S(1)} %constant_dynamic-update-slice_fusion.7, bf16[3072,256]{1,0:T(8,128)(2,1)} %collective-permute-done.1), kind=kLoop, calls=%fused_computation.22 | loop fusion | bytes 3145728
  117.2 0.2 constant_dynamic-update-slice_fusion.5
  117.5 1.6 %constant_dynamic-update-slice_fusion.4 = bf16[3072,2048]{1,0:T(8,128)(2,1)S(1)} fusion(bf16[3072,2048]{1,0:T(8,128)(2,1)S(1)} %constant_dynamic-update-slice_fusion.5, bf16[1,3072,256]{2,1,0:T(8,128)(2,1)} %param.1), kind=kLoop, calls=%fused_computation.20 | loop fusion | bytes 3145728
  119.1 1.6 %constant_dynamic-update-slice_fusion.3 = bf16[3072,2048]{1,0:T(8,128)(2,1)S(1)} fusion(bf16[3072,2048]{1,0:T(8,128)(2,1)S(1)} %constant_dynamic-update-slice_fusion.4, bf16[3072,256]{1,0:T(8,128)(2,1)} %collective-permute-done.2), kind=kLoop, calls=%fused_computation.19 | loop fusion | bytes 3145728
  120.7 1.6 %constant_dynamic-update-slice_fusion.2 = bf16[3072,2048]{1,0:T(8,128)(2,1)S(1)} fusion(bf16[3072,2048]{1,0:T(8,128)(2,1)S(1)} %constant_dynamic-update-slice_fusion.3, bf16[3072,256]{1,0:T(8,128)(2,1)} %collective-permute-done.1), kind=kLoop, calls=%fused_computation.18 | loop fusion | bytes 3145728
  122.4 0.2 constant_dynamic-update-slice_fusion.1
  122.6 0.0 copy-done
  122.6 0.2 constant_dynamic-update-slice_fusion
  122.8 0.0 copy-start.1
  122.8 4.5 %copy-done.1 = bf16[3072,2048]{1,0:T(8,128)(2,1)} copy-done((bf16[3072,2048]{1,0:T(8,128)(2,1)}, bf16[3072,2048]{1,0:T(8,128)(2,1)S(1)}, u32[]{:S(2)}) %copy-start.1) | copy-done | bytes 12582936
  127.4 8.3 %fusion.2 = f32[1024,1024]{1,0:T(8,128)} fusion(bf16[3072,2048]{1,0:T(8,128)(2,1)S(1)} %constant_dynamic-update-slice_fusion, s32[]{:T(128)S(6)} %select_n.17), kind=kOutput, calls=%fused_computation.2 | convolution fusion | flops 6442450944 | bytes 10485764 | tf_op jit(solution)/shard_map/dot_general | solution.py:72
  135.7 9.4 %fusion.7 = bf16[1,3072,256]{2,1,0:T(8,128)(2,1)} fusion(bf16[3072,2048]{1,0:T(8,128)(2,1)} %copy-done.1, s32[]{:T(128)S(6)} %select_n.17, f32[1024,1024]{1,0:T(8,128)} %fusion.2, s32[]{:T(128)S(6)} %select_n.18, s32[256]{0:T(256)S(1)} %iota_add_fusion), kind=kOutput, calls=%fused_computation.5 | convolution fusion | flops 2151677952 | bytes 14158336 | tf_op jit(solution)/shard_map/dot_general | solution.py:82
  (1 shorter events, 0.0 us)
Async XLA Ops:
  0.0 122.6 %copy-start = (bf16[1,3072,256]{2,1,0:T(8,128)(2,1)S(1)}, bf16[1,3072,256]{2,1,0:T(8,128)(2,1)}, u32[]{:S(2)}) copy-start(bf16[1,3072,256]{2,1,0:T(8,128)(2,1)} %param.1) | copy-start | bytes 4718596
  0.0 39.7 %collective-permute-start = (bf16[3072,256]{1,0:T(8,128)(2,1)}, bf16[3072,256]{1,0:T(8,128)(2,1)S(1)}, u32[]{:S(2)}, u32[]{:S(2)}) collective-permute-start(bf16[3072,256]{1,0:T(8,128)(2,1)} %bitcast.5), channel_id=1, source_target_pairs={{0,4},{4,8},{8,12},{12,0},{1,5},{5,9},{9,13},{13,1},{2,6},{6,10},{... | collective-permute-start | bytes 4718600 | tf_op jit(solution)/shard_map/ppermute | solution.py:68
  39.7 37.5 %collective-permute-start.1 = (bf16[3072,256]{1,0:T(8,128)(2,1)S(1)}, bf16[3072,256]{1,0:T(8,128)(2,1)}, u32[]{:S(2)}, u32[]{:S(2)}) collective-permute-start(bf16[3072,256]{1,0:T(8,128)(2,1)S(1)} %collective-permute-done), channel_id=1, source_target_pairs={{0,4},{4,8},{8,12},{12,0},{1,5},{5,9},{9,13},{13,1},{2,6},{6,10},{... | collective-permute-start | bytes 4718600 | tf_op jit(solution)/shard_map/ppermute | solution.py:68
  77.2 36.8 %collective-permute-start.2 = (bf16[3072,256]{1,0:T(8,128)(2,1)}, bf16[3072,256]{1,0:T(8,128)(2,1)}, u32[]{:S(2)}, u32[]{:S(2)}) collective-permute-start(bf16[3072,256]{1,0:T(8,128)(2,1)} %collective-permute-done.1), channel_id=1, source_target_pairs={{0,4},{4,8},{8,12},{12,0},{1,5},{5,9},{9,13},{13,1},{2,6},{6,10},{... | collective-permute-start | bytes 4718600 | tf_op jit(solution)/shard_map/ppermute | solution.py:68
  122.8 4.6 %copy-start.1 = (bf16[3072,2048]{1,0:T(8,128)(2,1)}, bf16[3072,2048]{1,0:T(8,128)(2,1)S(1)}, u32[]{:S(2)}) copy-start(bf16[3072,2048]{1,0:T(8,128)(2,1)S(1)} %constant_dynamic-update-slice_fusion) | copy-start | bytes 37748740
